TPU v7x, 256 devices: a whole 4x4x8 slice. The times are simulated.
256 devices in a mesh: leaf: 256 (over y, z, x, core).
Axes of the slice: x: 4, y: 4, z: 8, core: 2. Of those that a mesh axis runs over, the one named last changes fastest.
Arguments:
- points: bfloat16 [64, 1048576], P(None, 'leaf'), may hold values from -0.8 to 0.8
- leaf_order: int32 [1048576], P('leaf'), may hold values from 0 to 4095, as said below
- near_pairs: int32 [2048, 4], P('leaf'), may hold values from -1 to 2047, as said below
- solution: float32 [64, 1048576], P(None, 'leaf'), may hold values from -6 to 6
- residual: float32 [64, 1048576], P(None, 'leaf'), may hold values from -44 to 44
- direction: float32 [64, 1048576], P(None, 'leaf'), may hold values from -44 to 44
- skeleton_basis: bfloat16 [256, 1048576], P(None, 'leaf'), may hold values from -0.1875 to 0.1875
- transfers: float32 [1280, 256, 256], P('leaf'), may hold values from -0.375 to 0.375
- couplings: float32 [6, 256, 256], replicated, may hold values from -0.375 to 0.375
Outputs:
- new_solution: float32 [64, 1048576], P(None, 'leaf')
- new_residual: float32 [64, 1048576], P(None, 'leaf')
- new_direction: float32 [64, 1048576], P(None, 'leaf')
Inputs may be any that keep to these rules, and one draw needn't show every extreme that they name: `leaf_order`: the entries of each slab's 4096 positions are a permutation of 0 to 4095. `near_pairs`: row a lists 4 different later leaves: the first is always a + 1, the others lie among a + 2 to a + 8; -1 stands where that leaf would lie past the last leaf.
All inputs are finite; a program needn't handle non-finite values.
Results may differ from a plain program's by a relative error of at most 0.0034.
The roundings to bfloat16 on the way count: a program that leaves them out, or rounds other values in their place, can miss the bound.
Values may be sent and summed in bfloat16 or wider, within the bound.
No kernel may reach another device: no remote copies, remote signals or barrier semaphores. Data moves between devices by JAX's collectives and lax.ppermute only.
A program may use at most 128 MiB of HBM per device.

v0:
```python
import jax
import jax.numpy as jnp
from jax import lax
from jax.sharding import PartitionSpec as P

SHARPNESS = 2.0
EPSILON = 1e-06
HIGHEST = lax.Precision.HIGHEST


def swapped(block, axis, apart):
    count = lax.axis_size(axis)
    route = []
    for low in range(count):
        high = low | 1 << apart
        if high != low and high < count:
            route += [(low, high), (high, low)]
    return lax.ppermute(block, axis, route)


def passed_along(x, axis, by):
    peers = lax.axis_size(axis)
    pairs = [(i, i + by) for i in range(peers) if 0 <= i + by < peers]
    return lax.ppermute(x, axis, pairs)


def couple(level_total, weights):
    halfway = jnp.dot(level_total, weights, precision=HIGHEST)
    return lax.dot_general(halfway, weights, (((1,), (1,)), ((), ())), precision=HIGHEST)


def leaf_terms(win_pts, win_vec, win_sq, sources, others, src_weight, other_weight):

    def per_leaf(pieces):
        source, partner, weight_src, weight_oth = pieces
        source_pts = lax.dynamic_index_in_dim(win_pts, source, 1, keepdims=False)
        source_sq = lax.dynamic_index_in_dim(win_sq, source, 0, keepdims=False)
        source_val = lax.dynamic_index_in_dim(win_vec, source, 1, keepdims=False)
        partner_pts = jnp.take(win_pts, partner, axis=1)
        partner_sq = jnp.take(win_sq, partner, axis=0)
        cross_dot = jnp.einsum(
            "dk,dnj->nkj", source_pts, partner_pts, preferred_element_type=jnp.float32
        )
        distance = source_sq[None, :, None] + partner_sq[:, None, :] - 2.0 * cross_dot
        kernel_tile = jnp.exp(-SHARPNESS * distance).astype(jnp.bfloat16)
        to_partner = (
            jnp.einsum("nkj,rk->nrj", kernel_tile, source_val, preferred_element_type=jnp.float32)
            * weight_oth[:, None, None]
        )
        partner_val = jnp.take(win_vec, partner, axis=1)
        to_source = jnp.einsum(
            "nkj,rnj->nrk", kernel_tile, partner_val, preferred_element_type=jnp.float32
        )
        to_source = jnp.sum(to_source * weight_src[:, None, None], axis=0)
        return (to_source, to_partner)

    return lax.map(per_leaf, (sources, others, src_weight, other_weight))


def spread_rows(targets, contribs, slot_count):
    onehot = (targets[..., None] == jnp.arange(slot_count, dtype=jnp.int32)).astype(jnp.float32)
    return jnp.einsum("anw,anrj->rwj", onehot, contribs, precision=HIGHEST)


def local(
    points,
    leaf_order,
    near_pairs,
    solution,
    residual,
    direction,
    skeleton_basis,
    transfers,
    couplings,
):
    tree_depth = transfers.shape[0]
    leaf_count = near_pairs.shape[0]
    coord_count = points.shape[0]
    rhs_count = direction.shape[0]
    slab_points = points.shape[1]
    leaf_size = slab_points // leaf_count
    first_leaf = lax.axis_index("leaf") * leaf_count
    has_prior = lax.axis_index("leaf") > 0
    tree_points = jnp.take(points, leaf_order, axis=1)
    p_half = direction.astype(jnp.bfloat16)
    stacked = jnp.concatenate([tree_points, p_half], axis=0)
    level_skel = jnp.einsum("ri,ci->rc", p_half, skeleton_basis, preferred_element_type=jnp.float32)
    skeletons = [level_skel]
    for level_idx in range(tree_depth):
        level_skel = jnp.dot(level_skel, transfers[level_idx], precision=HIGHEST)
        skeletons.append(level_skel)
    local_norm = jnp.sum(residual * residual, axis=1)
    top_total, old_norm = lax.psum((skeletons[tree_depth], local_norm), "leaf")
    running = jnp.stack(skeletons[:tree_depth])
    totals = []
    for level_bit in range(tree_depth):
        running = running + swapped(running, "leaf", level_bit)
        totals.append(running[0])
        running = running[1:]
    descent = couple(top_total, couplings[tree_depth])
    for level_idx in reversed(range(tree_depth)):
        descent = lax.dot_general(
            descent, transfers[level_idx], (((1,), (1,)), ((), ())), precision=HIGHEST
        ) + couple(totals[level_idx], couplings[level_idx])
    far = jnp.dot(descent.astype(jnp.bfloat16), skeleton_basis, preferred_element_type=jnp.float32)
    local_valid = near_pairs >= 0
    prior_lists = passed_along(near_pairs, "leaf", 1)
    prior_valid = (prior_lists >= 0) & has_prior
    own_slots = first_leaf + jnp.arange(leaf_count, dtype=jnp.int32)
    incoming = jnp.sum(
        ((near_pairs[..., None] == own_slots) & local_valid[..., None]).astype(jnp.int32),
        axis=(0, 1),
    )
    incoming = incoming + jnp.sum(
        ((prior_lists[..., None] == own_slots) & prior_valid[..., None]).astype(jnp.int32),
        axis=(0, 1),
    )
    pair_totals = jnp.sum(local_valid.astype(jnp.int32), axis=1) + incoming
    self_weight = (1 + pair_totals).astype(jnp.float32)
    valid_float = local_valid.astype(jnp.float32)
    own_index = jnp.arange(leaf_count, dtype=jnp.int32)
    ahead = passed_along(stacked, "leaf", -1)
    window = jnp.concatenate([stacked, ahead], axis=1)
    slot_count = window.shape[1] // leaf_size
    window = window.reshape(coord_count + rhs_count, slot_count, leaf_size)
    win_pts = window[:coord_count]
    win_vec = window[coord_count:]
    win_sq = jnp.sum(jnp.square(win_pts.astype(jnp.float32)), axis=0)
    partner_slots = jnp.where(local_valid, near_pairs - first_leaf, own_index[:, None])
    others = jnp.concatenate([own_index[:, None], partner_slots], axis=1)
    src_weight = jnp.concatenate([self_weight[:, None], valid_float], axis=1)
    zero_column = jnp.zeros((leaf_count, 1), jnp.float32)
    other_weight = jnp.concatenate([zero_column, valid_float], axis=1)
    to_source, to_partner = leaf_terms(
        win_pts, win_vec, win_sq, own_index, others, src_weight, other_weight
    )
    window_sum = spread_rows(others, to_partner, slot_count) + spread_rows(
        own_index[:, None], to_source[:, None], slot_count
    )
    near_local = window_sum[:, :leaf_count].reshape(rhs_count, slab_points)
    outgoing = window_sum[:, leaf_count:].reshape(rhs_count, slab_points)
    near = near_local + passed_along(outgoing.astype(jnp.bfloat16), "leaf", 1).astype(
        outgoing.dtype
    )
    image = direction + near + far
    curve_sum = lax.psum(jnp.sum(direction * image, axis=1), "leaf")
    step_size = old_norm / (curve_sum + EPSILON)
    new_residual = residual - step_size[:, None] * image
    new_norm = lax.psum(jnp.sum(new_residual * new_residual, axis=1), "leaf")
    new_solution = solution + step_size[:, None] * direction
    ratio = new_norm / (old_norm + EPSILON)
    new_direction = new_residual + ratio[:, None] * direction
    return (new_solution, new_residual, new_direction)


def solution(mesh):
    in_specs = (
        P(None, "leaf"),
        P("leaf"),
        P("leaf", None),
        P(None, "leaf"),
        P(None, "leaf"),
        P(None, "leaf"),
        P(None, "leaf"),
        P("leaf", None, None),
        P(),
    )
    out_specs = (P(None, "leaf"), P(None, "leaf"), P(None, "leaf"))
    return jax.shard_map(local, mesh=mesh, in_specs=in_specs, out_specs=out_specs, check_vma=False)
```

profile of v0, /device:TPU:1, one launch (start us, length us, event | category | flops | bytes accessed | tf_op | source)
XLA Modules:
  0.0 719.6 jit_solution(17174719818674308560)
XLA Ops:
  8.1 4.5 collective-permute-start.1
  19.6 15.0 %gather_fusion.3 = bf16[4096,64]{1,0:T(8,128)(2,1)} fusion(bf16[64,4096]{0,1:T(8,128)(2,1)S(1)} %copy.30, s32[4096]{0:T(1024)S(1)} %fusion.91), kind=kCustom, calls=%fused_computation.3 | custom fusion | bytes 1064960 | tf_op jit(solution)/shard_map/jit(_take)/gather | solution.py:84
  34.7 3.5 select_bitcast_fusion
  45.3 216.7 %all-reduce.4.cloned.1.call-done = f32[64,256]{1,0:T(8,128)} async-done(((f32[64,256]{1,0:T(8,128)}), f32[64,256]{1,0:T(8,128)}) %all-reduce.4.cloned.1.call-update) | async-done | bytes 65552 | tf_op jit(solution)/shard_map/psum | solution.py:93
  268.0 6.0 collective-permute-done.4
  275.2 6.3 collective-permute-done.5
  286.1 3.7 collective-permute-done.7
  295.4 2.7 fusion.97
  298.1 2.7 copy.38
  300.8 2.7 copy.37
  303.5 230.2 %while.12 = (s32[]{:T(128)}, f32[8,64,512]{2,0,1:T(8,128)}, f32[8,5,64,512]{3,0,1,2:T(8,128)}, s32[8,5]{1,0:T(8,128)S(1)}, bf16[64,16,512]{2,0,1:T(8,128)(2,1)},...) while((s32[]{:T(128)}, f32[8,64,512]{2,0,1:T(8,128)}, ...), condition=%wide.region_8.10_spmd, body=%wide.region_6.0_spmd.sunk | while | flops 510661184 | bytes 13959699 | solution.py:57
  316.4 3.7 dynamic_update_slice.10
  320.1 12.1 %dynamic_update_slice.11 = f32[8,5,64,512]{3,0,1,2:T(8,128)} dynamic-update-slice(f32[8,5,64,512]{3,0,1,2:T(8,128)} %get-tuple-element.212, f32[1,5,64,512]{3,0,1,2:T(1,128)S(1)} %copy.59, s32[]{:T(128)S(6)} %copy.65, s32[]{:T(128)} %constant.56.clone.1..sunk, s32[]{:T(128)} %constant.56.clone.1..sunk, s32[]{:T(128)} %constant.56.clone.1..sunk) | dynamic-update-slice | bytes 1310724 | tf_op jit(solution)/shard_map/while/body/jit(dynamic_update_index_in_dim)/dynamic_update_slice | solution.py:57
  345.2 3.7 dynamic_update_slice.10
  348.9 12.1 %dynamic_update_slice.11 = f32[8,5,64,512]{3,0,1,2:T(8,128)} dynamic-update-slice(f32[8,5,64,512]{3,0,1,2:T(8,128)} %get-tuple-element.212, f32[1,5,64,512]{3,0,1,2:T(1,128)S(1)} %copy.59, s32[]{:T(128)S(6)} %copy.65, s32[]{:T(128)} %constant.56.clone.1..sunk, s32[]{:T(128)} %constant.56.clone.1..sunk, s32[]{:T(128)} %constant.56.clone.1..sunk) | dynamic-update-slice | bytes 1310724 | tf_op jit(solution)/shard_map/while/body/jit(dynamic_update_index_in_dim)/dynamic_update_slice | solution.py:57
  373.9 3.7 dynamic_update_slice.10
  377.7 12.1 %dynamic_update_slice.11 = f32[8,5,64,512]{3,0,1,2:T(8,128)} dynamic-update-slice(f32[8,5,64,512]{3,0,1,2:T(8,128)} %get-tuple-element.212, f32[1,5,64,512]{3,0,1,2:T(1,128)S(1)} %copy.59, s32[]{:T(128)S(6)} %copy.65, s32[]{:T(128)} %constant.56.clone.1..sunk, s32[]{:T(128)} %constant.56.clone.1..sunk, s32[]{:T(128)} %constant.56.clone.1..sunk) | dynamic-update-slice | bytes 1310724 | tf_op jit(solution)/shard_map/while/body/jit(dynamic_update_index_in_dim)/dynamic_update_slice | solution.py:57
  402.7 3.7 dynamic_update_slice.10
  406.5 12.1 %dynamic_update_slice.11 = f32[8,5,64,512]{3,0,1,2:T(8,128)} dynamic-update-slice(f32[8,5,64,512]{3,0,1,2:T(8,128)} %get-tuple-element.212, f32[1,5,64,512]{3,0,1,2:T(1,128)S(1)} %copy.59, s32[]{:T(128)S(6)} %copy.65, s32[]{:T(128)} %constant.56.clone.1..sunk, s32[]{:T(128)} %constant.56.clone.1..sunk, s32[]{:T(128)} %constant.56.clone.1..sunk) | dynamic-update-slice | bytes 1310724 | tf_op jit(solution)/shard_map/while/body/jit(dynamic_update_index_in_dim)/dynamic_update_slice | solution.py:57
  431.5 3.7 dynamic_update_slice.10
  435.2 12.1 %dynamic_update_slice.11 = f32[8,5,64,512]{3,0,1,2:T(8,128)} dynamic-update-slice(f32[8,5,64,512]{3,0,1,2:T(8,128)} %get-tuple-element.212, f32[1,5,64,512]{3,0,1,2:T(1,128)S(1)} %copy.59, s32[]{:T(128)S(6)} %copy.65, s32[]{:T(128)} %constant.56.clone.1..sunk, s32[]{:T(128)} %constant.56.clone.1..sunk, s32[]{:T(128)} %constant.56.clone.1..sunk) | dynamic-update-slice | bytes 1310724 | tf_op jit(solution)/shard_map/while/body/jit(dynamic_update_index_in_dim)/dynamic_update_slice | solution.py:57
  460.3 3.7 dynamic_update_slice.10
  464.0 12.1 %dynamic_update_slice.11 = f32[8,5,64,512]{3,0,1,2:T(8,128)} dynamic-update-slice(f32[8,5,64,512]{3,0,1,2:T(8,128)} %get-tuple-element.212, f32[1,5,64,512]{3,0,1,2:T(1,128)S(1)} %copy.59, s32[]{:T(128)S(6)} %copy.65, s32[]{:T(128)} %constant.56.clone.1..sunk, s32[]{:T(128)} %constant.56.clone.1..sunk, s32[]{:T(128)} %constant.56.clone.1..sunk) | dynamic-update-slice | bytes 1310724 | tf_op jit(solution)/shard_map/while/body/jit(dynamic_update_index_in_dim)/dynamic_update_slice | solution.py:57
  489.0 3.7 dynamic_update_slice.10
  492.8 12.1 %dynamic_update_slice.11 = f32[8,5,64,512]{3,0,1,2:T(8,128)} dynamic-update-slice(f32[8,5,64,512]{3,0,1,2:T(8,128)} %get-tuple-element.212, f32[1,5,64,512]{3,0,1,2:T(1,128)S(1)} %copy.59, s32[]{:T(128)S(6)} %copy.65, s32[]{:T(128)} %constant.56.clone.1..sunk, s32[]{:T(128)} %constant.56.clone.1..sunk, s32[]{:T(128)} %constant.56.clone.1..sunk) | dynamic-update-slice | bytes 1310724 | tf_op jit(solution)/shard_map/while/body/jit(dynamic_update_index_in_dim)/dynamic_update_slice | solution.py:57
  517.8 3.7 dynamic_update_slice.10
  521.6 12.1 %dynamic_update_slice.11 = f32[8,5,64,512]{3,0,1,2:T(8,128)} dynamic-update-slice(f32[8,5,64,512]{3,0,1,2:T(8,128)} %get-tuple-element.212, f32[1,5,64,512]{3,0,1,2:T(1,128)S(1)} %copy.59, s32[]{:T(128)S(6)} %copy.65, s32[]{:T(128)} %constant.56.clone.1..sunk, s32[]{:T(128)} %constant.56.clone.1..sunk, s32[]{:T(128)} %constant.56.clone.1..sunk) | dynamic-update-slice | bytes 1310724 | tf_op jit(solution)/shard_map/while/body/jit(dynamic_update_index_in_dim)/dynamic_update_slice | solution.py:57
  536.1 4.8 fusion.24
  541.1 6.3 collective-permute-start.2
  555.0 77.8 %all-reduce.1 = (f32[64]{0:T(128)S(1)}, f32[64]{0:T(128)S(1)}) all-reduce(f32[64]{0:T(128)S(1)} %multiply_reduce_fusion.3, f32[64]{0:T(128)S(1)} %get-tuple-element.126), channel_id=1, replica_groups=mesh['leaf'=256] {'leaf'}, use_global_device_ids=true, to_apply=%region_1.2 | all-reduce | flops 128 | bytes 1024 | tf_op jit(solution)/shard_map/psum | solution.py:93
  632.8 4.2 multiply_reduce_fusion.1
  637.0 73.3 %psum.31 = f32[64]{0:T(128)S(1)} all-reduce(f32[64]{0:T(128)S(1)} %get-tuple-element.105), channel_id=1, replica_groups=mesh['leaf'=256] {'leaf'}, use_global_device_ids=true, to_apply=%region_13.15 | all-reduce | flops 64 | bytes 512 | tf_op jit(solution)/shard_map/psum | solution.py:149
  (235 shorter events, 130.6 us)
Async XLA Ops:
  7.2 7.2 copy-start
  7.2 254.9 %all-reduce.4.cloned.1.call-start = ((), (), s32[]{:S(2)}) async-start(), calls=%async_computation | async-start | bytes 131072 | tf_op jit(solution)/shard_map/psum | solution.py:93
  8.1 36.8 %collective-permute-start.1 = (s32[8,4]{1,0:T(8,128)S(1)}, s32[8,4]{1,0:T(8,128)S(1)}, u32[]{:S(2)}, u32[]{:S(2)}) collective-permute-start(s32[8,4]{1,0:T(8,128)S(1)} %copy.28), channel_id=1, source_target_pairs={{0,1},{1,2},{2,3},{3,4},{4,5},{5,6},{6,7},{7,8},{8,9},{9,10},{10,1... | collective-permute-start | bytes 392 | tf_op jit(solution)/shard_map/ppermute | solution.py:24
  14.3 2.2 copy-start.1
  14.3 1.7 copy-start.8
  14.4 3.7 copy-start.11
  18.0 246.8 %collective-permute-start.3 = (f32[5,64,256]{2,1,0:T(8,128)S(1)}, f32[5,64,256]{2,1,0:T(8,128)}, u32[]{:S(2)}, u32[]{:S(2)}) collective-permute-start(f32[5,64,256]{2,1,0:T(8,128)S(1)} %get-tuple-element.124), channel_id=1, source_target_pairs={{0,1},{1,0},{2,3},{3,2},{4,5},{5,4},{6,7},{7,6},{8,9},{9,8},{10,11... | collective-permute-start | bytes 983048 | tf_op jit(solution)/shard_map/ppermute | solution.py:18
  34.7 4.4 copy-start.2
  38.1 1.0 copy-start.4
  39.1 5.9 copy-start.12
  40.7 251.7 %collective-permute-start = (bf16[128,4096]{0,1:T(8,128)(2,1)}, bf16[128,4096]{0,1:T(8,128)(2,1)}, u32[]{:S(2)}, u32[]{:S(2)}) collective-permute-start(bf16[128,4096]{0,1:T(8,128)(2,1)} %pad_maximum_fusion.1), channel_id=1, source_target_pairs={{1,0},{2,1},{3,2},{4,3},{5,4},{6,5},{7,6},{8,7},{9,8},{10,9},{11,1... | collective-permute-start | bytes 3145736 | tf_op jit(solution)/shard_map/ppermute | solution.py:24
  262.1 5.7 copy-start.7
  265.8 8.2 %collective-permute-start.4 = (f32[4,64,256]{2,1,0:T(8,128)S(1)}, f32[4,64,256]{2,1,0:T(8,128)S(1)}, u32[]{:S(2)}, u32[]{:S(2)}) collective-permute-start(f32[4,64,256]{2,1,0:T(8,128)S(1)} %slice.118), channel_id=1, source_target_pairs={{0,2},{2,0},{1,3},{3,1},{4,6},{6,4},{5,7},{7,5},{8,10},{10,8},{9,1... | collective-permute-start | bytes 786440 | tf_op jit(solution)/shard_map/ppermute | solution.py:18
  274.0 16.5 %copy-start.9 = (f32[5,256,256]{2,1,0:T(8,128)S(1)}, f32[5,256,256]{2,1,0:T(8,128)}, u32[]{:S(2)}) copy-start(f32[5,256,256]{2,1,0:T(8,128)} %param.20) | copy-start | bytes 3932164
  274.1 7.4 %collective-permute-start.5 = (f32[3,64,256]{2,1,0:T(8,128)S(1)}, f32[3,64,256]{2,1,0:T(8,128)S(1)}, u32[]{:S(2)}, u32[]{:S(2)}) collective-permute-start(f32[3,64,256]{2,1,0:T(8,128)S(1)} %slice.119), channel_id=1, source_target_pairs={{0,4},{4,0},{1,5},{5,1},{2,6},{6,2},{3,7},{7,3},{8,12},{12,8},{9,1... | collective-permute-start | bytes 589832 | tf_op jit(solution)/shard_map/ppermute | solution.py:18
  281.5 10.8 %copy-start.5 = (bf16[64,4096]{0,1:T(8,128)(2,1)S(1)}, bf16[64,4096]{0,1:T(8,128)(2,1)}, u32[]{:S(2)}) copy-start(bf16[64,4096]{0,1:T(8,128)(2,1)} %copy-done.4) | copy-start | bytes 1572868
  281.6 4.0 collective-permute-start.6
  285.6 4.3 collective-permute-start.7
  541.1 12.2 %collective-permute-start.2 = (bf16[64,4096]{1,0:T(8,128)(2,1)S(1)}, bf16[64,4096]{1,0:T(8,128)(2,1)S(1)}, u32[]{:S(2)}, u32[]{:S(2)}) collective-permute-start(bf16[64,4096]{1,0:T(8,128)(2,1)S(1)} %bitcast.211), channel_id=1, source_target_pairs={{0,1},{1,2},{2,3},{3,4},{4,5},{5,6},{6,7},{7,8},{8,9},{9,10},{10,1... | collective-permute-start | bytes 1572872 | tf_op jit(solution)/shard_map/ppermute | solution.py:24
  551.3 1.9 copy-start.3
  552.1 2.9 copy-start.6
  553.3 1.7 copy-start.10
Sparse Core Ops, SparseCore 0:
  18.1 243.9 all-reduce.3
where the time goes:
time: 725 us; the launch traced here: 720 us
  waiting for transfers between devices  236 us (33%)
  local copies, waits for them, and re-layouts  203 us (28%)
  blocking collectives  151 us (21%)
  matrix products  62.8 us (9%)
  other arithmetic  18.4 us (3%)
  loops' own time  17.3 us (2%)
  starting transfers between devices  16.7 us (2%)
  between operations  14.5 us (2%)
    psum x1, waiting for transfers between devices, local(): top_total, old_norm = lax.psum((skeletons[tree_depth], local_norm), 'leaf')  217 us
    dynamic_update_slice x32, local copies, waits for them, and re-layouts, leaf_terms(): return lax.map(per_leaf, (sources, others, src_weight, other_weight))  133 us
    psum x1, blocking collectives, local(): top_total, old_norm = lax.psum((skeletons[tree_depth], local_norm), 'leaf')  77.8 us
    psum x1, blocking collectives, local(): new_norm = lax.psum(jnp.sum(new_residual * new_residual, axis=1), 'leaf')  73.3 us
    dot_general x8, matrix products, per_leaf(): jnp.einsum('dk,dnj->nkj', source_pts, partner_pts, preferred_element_type...  21 us
    ppermute x5, waiting for transfers between devices, swapped(): return lax.ppermute(block, axis, route)  18.1 us
    another operation x1, loops' own time, leaf_terms(): return lax.map(per_leaf, (sources, others, src_weight, other_weight))  17.3 us
    gather x1, local copies, waits for them, and re-layouts, local(): tree_points = jnp.take(points, leaf_order, axis=1)  15 us
  transfers between devices with their start and end apart: 9, of which 6 were waited for; matrix products, arithmetic and copies ran while one was open for 6% of the time, Pallas kernels for 0%

commit v1 on v0

v1 whole, which is shorter than its diff:
```python
import functools

import jax
import jax.numpy as jnp
from jax import lax
from jax.experimental import pallas as pl
from jax.experimental.pallas import tpu as pltpu
from jax.sharding import PartitionSpec as P

EPSILON = 1e-06
LOG2E = 1.4426950408889634
HIGHEST = lax.Precision.HIGHEST
LEAF = 512
DIM = 64
ROWS = 64
LANES = 128
NT = (((1,), (1,)), ((), ()))
VMEM = pl.BlockSpec(memory_space=pltpu.VMEM)
SMEM = pl.BlockSpec(memory_space=pltpu.SMEM)


def call(body, name, out_shape, in_specs, out_specs, scratch, limit, flops, args, aliases=None):
    return pl.pallas_call(
        body,
        name=name,
        out_shape=out_shape,
        in_specs=in_specs,
        out_specs=out_specs,
        scratch_shapes=scratch,
        input_output_aliases=aliases or {},
        compiler_params=pltpu.CompilerParams(vmem_limit_bytes=limit << 20),
        cost_estimate=pl.CostEstimate(flops=flops, bytes_accessed=1 << 20, transcendentals=0),
    )(*args)


def shape(dims, dtype=jnp.float32):
    return jax.ShapeDtypeStruct(dims, dtype)


def split_squares(x):
    total = -2.0 * jnp.sum(x * x, axis=0, keepdims=True)
    high = total.astype(jnp.bfloat16).astype(jnp.float32)
    rest = total - high
    middle = rest.astype(jnp.bfloat16).astype(jnp.float32)
    return high, middle, rest - middle


def side_rows(parts, first, width):
    row = lax.broadcasted_iota(jnp.int32, (8, width), 0)
    out = jnp.where(row < 6, 1.0, 0.0)
    for i, part in enumerate(parts):
        out = jnp.where(row == first + i, part, out)
    return out


def right_form(x, parts):
    width = x.shape[1]
    filler = jnp.zeros((LANES - DIM - 8, width), jnp.float32)
    rows = jnp.concatenate([4.0 * x, side_rows(parts, 3, width), filler], axis=0)
    return rows.astype(jnp.bfloat16)


def gather_body(order, points, direction, left, right, stack, rows, picked):
    count = points.shape[1]
    for c in range(0, count, LANES):
        block = points[:, c : c + LANES].astype(jnp.float32)
        rows[c : c + LANES, :DIM] = block.T
    stack[DIM:, :] = direction[...].astype(jnp.bfloat16)

    def pick(i, carry):
        for u in range(16):
            j = i * 16 + u
            picked[pl.ds(j, 1), :] = rows[pl.ds(order[j], 1), :]
        return carry

    lax.fori_loop(0, count // 16, pick, 0)
    for c in range(0, count, LANES):
        span = slice(c, c + LANES)
        x = picked[span, :DIM].T
        stack[:DIM, span] = x.astype(jnp.bfloat16)
        parts = split_squares(x)
        right[:, span] = right_form(x, parts)
        filler = jnp.zeros((LANES - DIM - 8, LANES), jnp.float32)
        rows_left = jnp.concatenate([x, side_rows(parts, 0, LANES), filler], axis=0)
        left[span, :] = rows_left.T.astype(jnp.bfloat16)


def gather(order, points, direction):
    count = points.shape[1]
    return call(
        gather_body,
        "gather",
        (
            shape((count, LANES), jnp.bfloat16),
            shape((LANES, count), jnp.bfloat16),
            shape((DIM + ROWS, count), jnp.bfloat16),
        ),
        [SMEM, VMEM, VMEM],
        (VMEM, VMEM, VMEM),
        [pltpu.VMEM((count, LANES), jnp.float32)] * 2,
        16,
        4 << 30,
        (order, points, direction),
    )


def prepare_body(stack, right):
    for c in range(0, stack.shape[1], LANES):
        span = slice(c, c + LANES)
        x = stack[:DIM, span].astype(jnp.float32)
        right[:, span] = right_form(x, split_squares(x))


def prepare(stack):
    return call(
        prepare_body,
        "prepare",
        shape((LANES, stack.shape[1]), jnp.bfloat16),
        [VMEM],
        VMEM,
        [],
        8,
        1 << 29,
        (stack,),
    )


def up_body(direction, basis, transfers, out):
    level = lax.dot_general(
        direction[...].astype(jnp.bfloat16), basis[...], NT, preferred_element_type=jnp.float32
    )
    out[0] = level
    for k in range(transfers.shape[0]):
        level = jnp.dot(level, transfers[k], precision=HIGHEST)
        out[k + 1] = level


def up(direction, basis, transfers):
    rank = basis.shape[0]
    depth = transfers.shape[0]
    return call(
        up_body,
        "up",
        shape((depth + 1, ROWS, rank)),
        [VMEM] * 3,
        VMEM,
        [],
        16,
        2 << 30,
        (direction, basis, transfers),
    )


def down_body(totals, top, transfers, couplings, out):
    depth = transfers.shape[0]

    def couple(total, weights):
        halfway = jnp.dot(total, weights, precision=HIGHEST)
        return lax.dot_general(halfway, weights, NT, precision=HIGHEST)

    descent = couple(top[...], couplings[depth])
    for k in reversed(range(depth)):
        descent = lax.dot_general(descent, transfers[k], NT, precision=HIGHEST) + couple(
            totals[k], couplings[k]
        )
    out[...] = descent.astype(jnp.bfloat16)


def down(totals, top, transfers, couplings):
    return call(
        down_body,
        "down",
        shape(top.shape, jnp.bfloat16),
        [VMEM] * 4,
        VMEM,
        [],
        16,
        2 << 30,
        (totals, top, transfers, couplings),
    )


def leaf_span(i):
    return pl.ds(pl.multiple_of(i * LEAF, LEAF), LEAF)


def tile(left, right, source, partner, out, slot):
    exponent = jnp.dot(
        left[leaf_span(source), :],
        right[:, leaf_span(partner)],
        preferred_element_type=jnp.float32,
    )
    out[slot] = jnp.exp2(exponent * LOG2E).astype(jnp.bfloat16)


def values(stack, i):
    return stack[DIM:, leaf_span(i)]


def self_body(pairs, prior, left, right, stack, acc, tiles, weight):
    leaves = pairs.shape[0]
    first = pairs[0, 0] - 1
    has_prior = first > 0
    for a in range(leaves):
        weight[a] = 1
    for a in range(leaves):
        for m in range(pairs.shape[1]):
            partner = pairs[a, m]
            slot = partner - first

            @pl.when(partner >= 0)
            def _(a=a):
                weight[a] += 1

            @pl.when((partner >= 0) & (slot < leaves))
            def _(slot=slot):
                weight[slot] += 1

            back = prior[a, m]

            @pl.when(has_prior & (back >= first))
            def _(back=back):
                weight[back - first] += 1

    half = acc.shape[0] // 2
    acc[half:] = jnp.zeros((half,) + acc.shape[1:], jnp.float32)

    def use(a, slot):
        product = jnp.dot(values(stack, a), tiles[slot], preferred_element_type=jnp.float32)
        acc[a] = product * weight[a].astype(jnp.float32)

    tile(left, right, 0, 0, tiles, 0)

    def step(t, carry):
        tile(left, right, t, t, tiles, lax.rem(t, 2))
        use(t - 1, lax.rem(t - 1, 2))
        return carry

    lax.fori_loop(1, leaves, step, 0)
    use(leaves - 1, (leaves - 1) % 2)


def self_terms(pairs, prior, left, right, stack):
    leaves = pairs.shape[0]
    return call(
        self_body,
        "self_terms",
        shape((2 * leaves, ROWS, LEAF)),
        [SMEM, SMEM, VMEM, VMEM, VMEM],
        VMEM,
        [pltpu.VMEM((2, LEAF, LEAF), jnp.bfloat16), pltpu.SMEM((leaves,), jnp.int32)],
        20,
        4 << 30,
        (pairs, prior, left, right, stack),
    )


def pair_body(crossing, piece, pieces, pairs, left, right, stack, other, given, *rest):
    if len(rest) == 4:
        acc, outgoing, tiles, listed = rest
    else:
        (acc, tiles, listed), outgoing = rest, None
    leaves, width = pairs.shape
    first = pairs[0, 0] - 1
    shift = leaves if crossing else 0

    def build(t, found):
        a = t // width
        slot = pairs[a, lax.rem(t, width)] - first
        wanted = (slot >= leaves) if crossing else ((slot >= 0) & (slot < leaves))

        @pl.when(wanted)
        def _():
            listed[0, found] = a
            listed[1, found] = slot - shift

        return found + jnp.where(wanted, 1, 0)

    found = lax.fori_loop(0, leaves * width, build, 0)
    low = found * piece // pieces
    high = found * (piece + 1) // pieces

    def use(t):
        a, b = listed[0, t], listed[1, t]
        block = tiles[lax.rem(t, 2)]
        acc[b + shift] += jnp.dot(values(stack, a), block, preferred_element_type=jnp.float32)
        acc[a] += lax.dot_general(
            values(other, b), block, NT, preferred_element_type=jnp.float32
        )

    def make(t):
        tile(left, right, listed[0, t], listed[1, t], tiles, lax.rem(t, 2))

    @pl.when(high > low)
    def _():
        make(low)

        def step(t, carry):
            make(t)
            use(t - 1)
            return carry

        lax.fori_loop(low + 1, high, step, 0)
        use(high - 1)

    if outgoing is not None:
        outgoing[...] = acc[leaves:].astype(jnp.bfloat16)


def pair_terms(crossing, piece, pieces, pairs, left, right, stack, other, acc):
    leaves, width = pairs.shape
    last = crossing and piece == pieces - 1
    outs = [shape(acc.shape)]
    if last:
        outs.append(shape((leaves, ROWS, LEAF), jnp.bfloat16))
    return call(
        functools.partial(pair_body, crossing, piece, pieces),
        "pairs_%d_%d" % (crossing, piece),
        tuple(outs),
        [SMEM] + [VMEM] * 5,
        (VMEM,) * len(outs),
        [
            pltpu.VMEM((2, LEAF, LEAF), jnp.bfloat16),
            pltpu.SMEM((2, leaves * width), jnp.int32),
        ],
        20,
        4 << 30,
        (pairs, left, right, stack, other, acc),
        {5: 0},
    )


def image_body(direction, residual, acc, arrived, half, basis, image, sums):
    leaves = arrived.shape[0]
    zero = jnp.zeros((ROWS, LANES), jnp.float32)
    curve = cross = energy = norm = zero
    for a in range(leaves):
        span = slice(a * LEAF, (a + 1) * LEAF)
        far = jnp.dot(half[...], basis[:, span], preferred_element_type=jnp.float32)
        d = direction[:, span]
        r = residual[:, span]
        value = d + (acc[a] + arrived[a].astype(jnp.float32)) + far
        image[:, span] = value
        for c in range(0, LEAF, LANES):
            part = slice(c, c + LANES)
            v, e, s = value[:, part], d[:, part], r[:, part]
            curve += e * v
            cross += s * v
            energy += v * v
            norm += s * s
    lane = lax.broadcasted_iota(jnp.int32, (ROWS, LANES), 1)
    packed = zero
    for i, total in enumerate((curve, cross, energy, norm)):
        packed = jnp.where(lane == i, jnp.sum(total, axis=1, keepdims=True), packed)
    rows = packed.T
    peers = sums.shape[0]
    upper = jnp.concatenate([rows[0:1], rows[1:2]], axis=1)
    lower = jnp.concatenate([rows[2:3], rows[3:4]], axis=1)
    sums[...] = jnp.broadcast_to(
        jnp.concatenate([upper, lower], axis=0)[None], (peers, 2, LANES)
    )


def image_terms(peers, direction, residual, acc, arrived, half, basis):
    return call(
        image_body,
        "image",
        (shape(direction.shape), shape((peers, 2, LANES))),
        [VMEM] * 6,
        (VMEM, VMEM),
        [],
        24,
        2 << 30,
        (direction, residual, acc, arrived, half, basis),
    )


def final_body(sums, solution, residual, direction, image, out_x, out_r, out_d):
    total = jnp.sum(sums[...], axis=0)
    columns = jnp.broadcast_to(total[:, None, :], (2, LANES, LANES))
    upper, lower = columns[0].T, columns[1].T
    curve, cross = upper[:ROWS], upper[ROWS:]
    energy, old = lower[:ROWS], lower[ROWS:]
    step = old / (curve + EPSILON)
    new = jnp.maximum(old - step * (2.0 * cross - step * energy), 0.0)
    ratio = new / (old + EPSILON)
    for c in range(0, solution.shape[1], LANES):
        span = slice(c, c + LANES)
        d = direction[:, span]
        out_x[:, span] = solution[:, span] + step * d
        left = residual[:, span] - step * image[:, span]
        out_r[:, span] = left
        out_d[:, span] = left + ratio * d


def final(sums, solution, residual, direction, image):
    peers = sums.shape[0]
    count = solution.shape[1]
    width = 1024
    block = pl.BlockSpec((ROWS, width), lambda i: (0, i))
    return pl.pallas_call(
        final_body,
        name="final",
        grid=(count // width,),
        out_shape=(shape(solution.shape),) * 3,
        in_specs=[pl.BlockSpec((peers, 2, LANES), lambda i: (0, 0, 0))] + [block] * 4,
        out_specs=(block,) * 3,
        compiler_params=pltpu.CompilerParams(vmem_limit_bytes=16 << 20),
        cost_estimate=pl.CostEstimate(flops=1 << 26, bytes_accessed=7 << 20, transcendentals=0),
    )(sums, solution, residual, direction, image)


def swapped(block, axis, apart):
    count = lax.axis_size(axis)
    return lax.ppermute(block, axis, [(i, i ^ (1 << apart)) for i in range(count)])


def passed_along(x, axis, by):
    peers = lax.axis_size(axis)
    pairs = [(i, i + by) for i in range(peers) if 0 <= i + by < peers]
    return lax.ppermute(x, axis, pairs)


def local(
    points,
    leaf_order,
    near_pairs,
    solution,
    residual,
    direction,
    skeleton_basis,
    transfers,
    couplings,
):
    peers = lax.axis_size("leaf")
    depth = transfers.shape[0]
    bits = peers.bit_length() - 1
    prior = passed_along(near_pairs, "leaf", 1)
    running = up(direction, skeleton_basis, transfers)
    left, right, stack = gather(leaf_order, points, direction)
    ahead = passed_along(stack, "leaf", -1)

    state = {}

    def near_piece(i):
        if i == 0:
            state["acc"] = self_terms(near_pairs, prior, left, right, stack)
        elif i <= 3:
            (state["acc"],) = pair_terms(
                0, i - 1, 3, near_pairs, left, right, stack, stack, state["acc"]
            )
        else:
            if i == 4:
                state["next"] = prepare(ahead)
            out = pair_terms(
                1, i - 4, 3, near_pairs, left, state["next"], stack, ahead, state["acc"]
            )
            state["acc"] = out[0]
            if len(out) > 1:
                state["outgoing"] = out[1]

    totals = []
    for bit in range(bits):
        running = running + swapped(running, "leaf", bit)
        if bit < depth:
            totals.append(running[0])
            running = running[1:]
        if bit < 7:
            near_piece(bit)
    top = running[0]
    arrived = passed_along(state["outgoing"], "leaf", 1)
    half = down(jnp.stack(totals), top, transfers, couplings)
    image, sums = image_terms(
        peers, direction, residual, state["acc"], arrived, half, skeleton_basis
    )
    gathered = lax.all_to_all(sums, "leaf", 0, 0, tiled=True)
    return final(gathered, solution, residual, direction, image)


def solution(mesh):
    in_specs = (
        P(None, "leaf"),
        P("leaf"),
        P("leaf", None),
        P(None, "leaf"),
        P(None, "leaf"),
        P(None, "leaf"),
        P(None, "leaf"),
        P("leaf", None, None),
        P(),
    )
    out_specs = (P(None, "leaf"), P(None, "leaf"), P(None, "leaf"))
    return jax.shard_map(local, mesh=mesh, in_specs=in_specs, out_specs=out_specs, check_vma=False)
```

time: 725 us -> 134 us (0.18)
  waiting for transfers between devices: 236 us -> 20.8 us
  local copies, waits for them, and re-layouts: 203 us -> 4.35 us
  blocking collectives: 151 us -> 26.3 us
  matrix products: 62.8 us -> 0 us
  Pallas kernels: 0 us -> 56.5 us
  other arithmetic: 18.4 us -> 0.21 us
  loops' own time: 17.3 us -> 0 us
  between operations: 14.5 us -> 0.98 us
  starting transfers between devices: 16.7 us -> 24.7 us
    psum x1 -> x0, waiting for transfers between devices: 217 us -> none  [local(): top_total, old_norm = lax.psum((skeletons[tree_depth], local_norm), 'leaf')]
    psum x2 -> x0, blocking collectives: 151 us -> none  [the longest x1 77.8 us: local(): top_total, old_norm = lax.psum((skeletons[tree_depth], local_norm), 'leaf')]
    dynamic_update_slice x32 -> x0, local copies, waits for them, and re-layouts: 133 us -> none  [leaf_terms(): return lax.map(per_leaf, (sources, others, src_weight, other_weight))]
    dot_general x50 -> x0, matrix products: 62.8 us -> none  [the longest x8 21 us: per_leaf(): jnp.einsum('dk,dnj->nkj', source_pts, partner_pts, preferred_element_type...]
    pallas_call x0 -> x13, Pallas kernels: none -> 56.5 us  [the longest x12 53.2 us: call(): pl.pallas_call(body, name=name, out_shape=out_shape, in_specs=in_specs, o...]
    gather x25 -> x0, local copies, waits for them, and re-layouts: 48.2 us -> none  [the longest x1 15 us: local(): tree_points = jnp.take(points, leaf_order, axis=1)]
    all_to_all x0 -> x1, blocking collectives: none -> 26.3 us  [local(): gathered = lax.all_to_all(sums, 'leaf', 0, 0, tiled=True)]
    another operation x1 -> x0, loops' own time: 17.3 us -> none  [leaf_terms(): return lax.map(per_leaf, (sources, others, src_weight, other_weight))]
  transfers between devices with their start and end apart: 9 -> 11, of which waited for: 6 -> 6; matrix products, arithmetic and copies ran while one was open for 6% -> 0% of each run, Pallas kernels for 0% -> 37%
where the time goes in v1:
time: 134 us
  Pallas kernels  56.5 us (42%)
  blocking collectives  26.3 us (20%)
  starting transfers between devices  24.7 us (18%)
  waiting for transfers between devices  20.8 us (16%)
  local copies, waits for them, and re-layouts  4.35 us (3%)
    pallas_call x12, Pallas kernels, call(): pl.pallas_call(body, name=name, out_shape=out_shape, in_specs=in_specs, o...  53.2 us
    all_to_all x1, blocking collectives, local(): gathered = lax.all_to_all(sums, 'leaf', 0, 0, tiled=True)  26.3 us
    ppermute x8, waiting for transfers between devices, swapped(): lax.ppermute(block, axis, [(i, i ^ 1 << apart) for i in range(count)])  20.8 us
    ppermute x8, starting transfers between devices, swapped(): lax.ppermute(block, axis, [(i, i ^ 1 << apart) for i in range(count)])  12.5 us
    ppermute x3, starting transfers between devices, passed_along(): return lax.ppermute(x, axis, pairs)  12.2 us
    unnamed x29, local copies, waits for them, and re-layouts  4.27 us
    pallas_call x1, Pallas kernels, final(): pl.pallas_call(final_body, name='final', grid=(count // width,), out_shap...  3.28 us
  transfers between devices with their start and end apart: 11, of which 6 were waited for; matrix products, arithmetic and copies ran while one was open for 0% of the time, Pallas kernels for 37%

profile of v1, /device:TPU:1, one launch (start us, length us, event | category | flops | bytes accessed | tf_op | source)
XLA Modules:
  0.0 133.9 jit_solution(13570266710193103141)
XLA Ops:
  0.6 1.2 copy-done
  1.9 1.6 %copy-done.4 = bf16[256,4096]{1,0:T(8,128)(2,1)S(1)} copy-done((bf16[256,4096]{1,0:T(8,128)(2,1)S(1)}, bf16[256,4096]{1,0:T(8,128)(2,1)}, u32[]{:S(2)}) %copy-start.4) | copy-done | bytes 2097176
  3.5 1.3 copy-done.7
  4.8 2.7 %up.1 = f32[6,64,256]{2,1,0:T(8,128)S(1)} custom-call(f32[64,4096]{1,0:T(8,128)S(1)} %copy-done, bf16[256,4096]{1,0:T(8,128)(2,1)S(1)} %copy-done.4, f32[5,256,256]{2,1,0:T(8,128)S(1)} %copy-done.7), custom_call_target="tpu_custom_call" | custom-call | flops 2147483648 | bytes 1048576 | tf_op jit(solution)/shard_map/up/pallas_call | solution.py:23
  7.5 3.3 %collective-permute-start.3 = (f32[6,64,256]{2,1,0:T(8,128)S(1)}, f32[6,64,256]{2,1,0:T(8,128)S(1)}, u32[]{:S(2)}, u32[]{:S(2)}) collective-permute-start(f32[6,64,256]{2,1,0:T(8,128)S(1)} %up.1), channel_id=1, source_target_pairs={{0,1},{1,0},{2,3},{3,2},{4,5},{5,4},{6,7},{7,6},{8,9},{9,8},{10,11... | collective-permute-start | bytes 1179656 | tf_op jit(solution)/shard_map/ppermute | solution.py:415
  10.9 1.9 %collective-permute-start.1 = (s32[8,4]{1,0:T(8,128)S(1)}, s32[8,4]{1,0:T(8,128)S(1)}, u32[]{:S(2)}, u32[]{:S(2)}) collective-permute-start(s32[8,4]{1,0:T(8,128)S(1)} %copy.25.pairs), channel_id=1, source_target_pairs={{0,1},{1,2},{2,3},{3,4},{4,5},{5,6},{6,7},{7,8},{8,9},{9,10},{10,1... | collective-permute-start | bytes 392 | tf_op jit(solution)/shard_map/ppermute | solution.py:421
  12.8 8.8 %gather.1 = (bf16[4096,128]{1,0:T(8,128)(2,1)S(1)}, bf16[128,4096]{1,0:T(8,128)(2,1)S(1)}, bf16[128,4096]{1,0:T(8,128)(2,1)S(1)}) custom-call(s32[4096]{0:T(1024)S(1)} %copy-done.10, bf16[64,4096]{1,0:T(8,128)(2,1)S(1)} %copy-done.9, f32[64,4096]{1,0:T(8,128)S(1)} %copy-done.1), custom_call_target="tpu_custom_call" | custom-call | flops 4294967296 | bytes 1048576 | tf_op jit(solution)/shard_map/gather/pallas_call | solution.py:23
  21.6 2.4 %collective-permute-start = (bf16[128,4096]{1,0:T(8,128)(2,1)S(1)}, bf16[128,4096]{1,0:T(8,128)(2,1)S(1)}, u32[]{:S(2)}, u32[]{:S(2)}) collective-permute-start(bf16[128,4096]{1,0:T(8,128)(2,1)S(1)} %get-tuple-element.11.stack.other), channel_id=1, source_target_pairs={{1,0},{2,1},{3,2},{4,3},{5,4},{6,5},{7,6},{8,7},{9,8},{10,9},{11,1... | collective-permute-start | bytes 3145736 | tf_op jit(solution)/shard_map/ppermute | solution.py:421
  24.0 5.5 %self_terms.1.given = f32[16,64,512]{2,1,0:T(8,128)S(1)} custom-call(s32[8,4]{1,0:T(8,128)S(1)} %copy.25.pairs, s32[8,4]{1,0:T(8,128)S(1)} %collective-permute-done.1.prior, bf16[4096,128]{1,0:T(8,128)(2,1)S(1)} %get-tuple-element.10.left, bf16[128,4096]{1,0:T(8,128)(2,1)S(1)} %get-tuple-element.12.right, bf16[128,4096]{1,0:T(8,128)(2,1)S(1)} %get-tuple-element.11.stack.other), custom_call_target="tpu_custom_call" | custom-call | flops 4294967296 | bytes 1048576 | tf_op jit(solution)/shard_map/self_terms/pallas_call | solution.py:23
  29.5 5.6 %pairs_0_0.1.given = f32[16,64,512]{2,1,0:T(8,128)S(1)} custom-call(s32[8,4]{1,0:T(8,128)S(1)} %copy.25.pairs, bf16[4096,128]{1,0:T(8,128)(2,1)S(1)} %get-tuple-element.10.left, bf16[128,4096]{1,0:T(8,128)(2,1)S(1)} %get-tuple-element.12.right, bf16[128,4096]{1,0:T(8,128)(2,1)S(1)} %get-tuple-element.11.stack.other, ...), custom_call_target="tpu_custom_call", output_to_operand_aliasing={{}: (5, {})} | custom-call | flops 4294967296 | bytes 1048576 | tf_op jit(solution)/shard_map/pairs_0_0/pallas_call | solution.py:23
  35.2 5.6 %pairs_0_1.1.given = f32[16,64,512]{2,1,0:T(8,128)S(1)} custom-call(s32[8,4]{1,0:T(8,128)S(1)} %copy.25.pairs, bf16[4096,128]{1,0:T(8,128)(2,1)S(1)} %get-tuple-element.10.left, bf16[128,4096]{1,0:T(8,128)(2,1)S(1)} %get-tuple-element.12.right, bf16[128,4096]{1,0:T(8,128)(2,1)S(1)} %get-tuple-element.11.stack.other, ...), custom_call_target="tpu_custom_call", output_to_operand_aliasing={{}: (5, {})} | custom-call | flops 4294967296 | bytes 1048576 | tf_op jit(solution)/shard_map/pairs_0_1/pallas_call | solution.py:23
  41.0 6.4 %pairs_0_2.1.given = f32[16,64,512]{2,1,0:T(8,128)S(1)} custom-call(s32[8,4]{1,0:T(8,128)S(1)} %copy.25.pairs, bf16[4096,128]{1,0:T(8,128)(2,1)S(1)} %get-tuple-element.10.left, bf16[128,4096]{1,0:T(8,128)(2,1)S(1)} %get-tuple-element.12.right, bf16[128,4096]{1,0:T(8,128)(2,1)S(1)} %get-tuple-element.11.stack.other, ...), custom_call_target="tpu_custom_call", output_to_operand_aliasing={{}: (5, {})} | custom-call | flops 4294967296 | bytes 1048576 | tf_op jit(solution)/shard_map/pairs_0_2/pallas_call | solution.py:23
  47.5 1.6 %collective-permute-done.4 = f32[5,64,256]{2,1,0:T(8,128)S(1)} collective-permute-done((f32[5,64,256]{2,1,0:T(8,128)S(1)}, f32[5,64,256]{2,1,0:T(8,128)S(1)}, u32[]{:S(2)}, u32[]{:S(2)}) %collective-permute-start.4) | collective-permute-done | bytes 327712 | tf_op jit(solution)/shard_map/ppermute | solution.py:415
  49.1 1.1 collective-permute-start.5
  50.2 8.4 %collective-permute-done.5 = f32[4,64,256]{2,1,0:T(8,128)S(1)} collective-permute-done((f32[4,64,256]{2,1,0:T(8,128)S(1)}, f32[4,64,256]{2,1,0:T(8,128)S(1)}, u32[]{:S(2)}, u32[]{:S(2)}) %collective-permute-start.5) | collective-permute-done | bytes 262176 | tf_op jit(solution)/shard_map/ppermute | solution.py:415
  58.6 0.1 collective-permute-start.6
  58.8 0.3 prepare.1.right
  59.1 4.1 %pairs_1_0.1.given = f32[16,64,512]{2,1,0:T(8,128)S(1)} custom-call(s32[8,4]{1,0:T(8,128)S(1)} %copy.25.pairs, bf16[4096,128]{1,0:T(8,128)(2,1)S(1)} %get-tuple-element.10.left, bf16[128,4096]{1,0:T(8,128)(2,1)S(1)} %prepare.1.right, bf16[128,4096]{1,0:T(8,128)(2,1)S(1)} %get-tuple-element.11.stack.other, ...), custom_call_target="tpu_custom_call", output_to_operand_aliasing={{}: (5, {})} | custom-call | flops 4294967296 | bytes 1048576 | tf_op jit(solution)/shard_map/pairs_1_0/pallas_call | solution.py:23
  63.1 1.2 collective-permute-done.6
  64.4 3.4 %collective-permute-start.7 = (f32[2,64,256]{2,1,0:T(8,128)S(1)}, f32[2,64,256]{2,1,0:T(8,128)S(1)}, u32[]{:S(2)}, u32[]{:S(2)}) collective-permute-start(f32[2,64,256]{2,1,0:T(8,128)S(1)} %slice.47), channel_id=1, source_target_pairs={{0,16},{1,17},{2,18},{3,19},{4,20},{5,21},{6,22},{7,23},{8,24},{9,... | collective-permute-start | bytes 393224 | tf_op jit(solution)/shard_map/ppermute | solution.py:415
  67.8 4.3 %pairs_1_1.1.given = f32[16,64,512]{2,1,0:T(8,128)S(1)} custom-call(s32[8,4]{1,0:T(8,128)S(1)} %copy.25.pairs, bf16[4096,128]{1,0:T(8,128)(2,1)S(1)} %get-tuple-element.10.left, bf16[128,4096]{1,0:T(8,128)(2,1)S(1)} %prepare.1.right, bf16[128,4096]{1,0:T(8,128)(2,1)S(1)} %get-tuple-element.11.stack.other, ...), custom_call_target="tpu_custom_call", output_to_operand_aliasing={{}: (5, {})} | custom-call | flops 4294967296 | bytes 1048576 | tf_op jit(solution)/shard_map/pairs_1_1/pallas_call | solution.py:23
  72.1 1.7 %collective-permute-done.7 = f32[2,64,256]{2,1,0:T(8,128)S(1)} collective-permute-done((f32[2,64,256]{2,1,0:T(8,128)S(1)}, f32[2,64,256]{2,1,0:T(8,128)S(1)}, u32[]{:S(2)}, u32[]{:S(2)}) %collective-permute-start.7) | collective-permute-done | bytes 131104 | tf_op jit(solution)/shard_map/ppermute | solution.py:415
  73.8 2.4 %collective-permute-start.8 = (f32[1,64,256]{2,1,0:T(8,128)S(1)}, f32[1,64,256]{2,1,0:T(8,128)S(1)}, u32[]{:S(2)}, u32[]{:S(2)}) collective-permute-start(f32[1,64,256]{2,1,0:T(8,128)S(1)} %slice.49), channel_id=1, source_target_pairs={{0,32},{1,33},{2,34},{3,35},{4,36},{5,37},{6,38},{7,39},{8,40},{9,... | collective-permute-start | bytes 196616 | tf_op jit(solution)/shard_map/ppermute | solution.py:415
  76.2 4.8 %collective-permute-done.8 = f32[1,64,256]{2,1,0:T(8,128)S(1)} collective-permute-done((f32[1,64,256]{2,1,0:T(8,128)S(1)}, f32[1,64,256]{2,1,0:T(8,128)S(1)}, u32[]{:S(2)}, u32[]{:S(2)}) %collective-permute-start.8) | collective-permute-done | bytes 65568 | tf_op jit(solution)/shard_map/ppermute | solution.py:415
  81.1 4.9 %pairs_1_2.1 = (f32[16,64,512]{2,1,0:T(8,128)S(1)}, bf16[8,64,512]{2,1,0:T(8,128)(2,1)S(1)}) custom-call(s32[8,4]{1,0:T(8,128)S(1)} %copy.25.pairs, bf16[4096,128]{1,0:T(8,128)(2,1)S(1)} %get-tuple-element.10.left, bf16[128,4096]{1,0:T(8,128)(2,1)S(1)} %prepare.1.right, ...), custom_call_target="tpu_custom_call", output_to_operand_aliasing={{0}: (5, {})} | custom-call | flops 4294967296 | bytes 1048576 | tf_op jit(solution)/shard_map/pairs_1_2/pallas_call | solution.py:23
  86.0 7.9 %collective-permute-start.2 = (bf16[8,64,512]{2,1,0:T(8,128)(2,1)S(1)}, bf16[8,64,512]{2,1,0:T(8,128)(2,1)S(1)}, u32[]{:S(2)}, u32[]{:S(2)}) collective-permute-start(bf16[8,64,512]{2,1,0:T(8,128)(2,1)S(1)} %get-tuple-element.14), channel_id=1, source_target_pairs={{0,1},{1,2},{2,3},{3,4},{4,5},{5,6},{6,7},{7,8},{8,9},{9,10},{10,1... | collective-permute-start | bytes 1572872 | tf_op jit(solution)/shard_map/ppermute | solution.py:421
  94.0 2.1 %collective-permute-start.10 = (f32[1,64,256]{2,1,0:T(8,128)S(1)}, f32[1,64,256]{2,1,0:T(8,128)S(1)}, u32[]{:S(2)}, u32[]{:S(2)}) collective-permute-start(f32[1,64,256]{2,1,0:T(8,128)S(1)} %add.30), channel_id=1, source_target_pairs={{0,128},{1,129},{2,130},{3,131},{4,132},{5,133},{6,134},{7,135},{8... | collective-permute-start | bytes 196616 | tf_op jit(solution)/shard_map/ppermute | solution.py:415
  96.1 3.1 %collective-permute-done.10 = f32[1,64,256]{2,1,0:T(8,128)S(1)} collective-permute-done((f32[1,64,256]{2,1,0:T(8,128)S(1)}, f32[1,64,256]{2,1,0:T(8,128)S(1)}, u32[]{:S(2)}, u32[]{:S(2)}) %collective-permute-start.10) | collective-permute-done | bytes 65568 | tf_op jit(solution)/shard_map/ppermute | solution.py:415
  99.2 4.0 %down.1.half = bf16[64,256]{1,0:T(8,128)(2,1)S(1)} custom-call(f32[5,64,256]{2,1,0:T(8,128)S(1)} %get-tuple-element.18.totals, f32[64,256]{1,0:T(8,128)S(1)} %add_bitcast_fusion.top, f32[5,256,256]{2,1,0:T(8,128)S(1)} %copy-done.8, f32[6,256,256]{2,1,0:T(8,128)S(1)} %copy-done.6), custom_call_target="tpu_custom_call" | custom-call | flops 2147483648 | bytes 1048576 | tf_op jit(solution)/shard_map/down/pallas_call | solution.py:23
  103.3 1.0 image.1
  104.3 26.3 %all_to_all.5.sums = f32[256,2,128]{2,1,0:T(2,128)S(1)} all-to-all(f32[256,2,128]{2,1,0:T(2,128)S(1)} %get-tuple-element.15), channel_id=1, replica_groups=mesh['leaf'=256] {'leaf'}, dimensions={0} | all-to-all | bytes 524288 | tf_op jit(solution)/shard_map/all_to_all | solution.py:476
  130.6 3.3 %final.1 = (f32[64,4096]{1,0:T(8,128)}, f32[64,4096]{1,0:T(8,128)}, f32[64,4096]{1,0:T(8,128)}) custom-call(f32[256,2,128]{2,1,0:T(2,128)S(1)} %all_to_all.5.sums, f32[64,4096]{1,0:T(8,128)S(1)} %copy-done.3, f32[64,4096]{1,0:T(8,128)S(1)} %copy-done.2, f32[64,4096]{1,0:T(8,128)S(1)} %copy-done.1, f32[64,4096]{1,0:T(8,128)S(1)} %get-tuple-element.16.image), custom_call_target="tpu_custom_call" | custom-call | flops 67108864 | bytes 7340032 | tf_op jit(solution)/shard_map/final/pallas_call | solution.py:401
  (46 shorter events, 0.6 us)
Async XLA Ops:
  0.6 1.2 copy-start
  1.9 1.6 %copy-start.4 = (bf16[256,4096]{1,0:T(8,128)(2,1)S(1)}, bf16[256,4096]{1,0:T(8,128)(2,1)}, u32[]{:S(2)}) copy-start(bf16[256,4096]{1,0:T(8,128)(2,1)} %basis.3) | copy-start | bytes 6291460
  3.4 1.3 copy-start.7
  4.8 6.0 %copy-start.11 = (s32[8,4]{0,1:T(4,128)S(1)}, s32[8,4]{0,1:T(4,128)}, u32[]{:S(2)}) copy-start(s32[8,4]{0,1:T(4,128)} %param.11) | copy-start | bytes 388
  4.8 8.0 %copy-start.1 = (f32[64,4096]{1,0:T(8,128)S(1)}, f32[64,4096]{1,0:T(8,128)}, u32[]{:S(2)}) copy-start(f32[64,4096]{1,0:T(8,128)} %direction.7) | copy-start | bytes 3145732
  4.8 8.0 %copy-start.9 = (bf16[64,4096]{1,0:T(8,128)(2,1)S(1)}, bf16[64,4096]{1,0:T(8,128)(2,1)}, u32[]{:S(2)}) copy-start(bf16[64,4096]{1,0:T(8,128)(2,1)} %points.1) | copy-start | bytes 1572868
  4.8 8.0 %copy-start.10 = (s32[4096]{0:T(1024)S(1)}, s32[4096]{0:T(1024)}, u32[]{:S(2)}) copy-start(s32[4096]{0:T(1024)} %order.1) | copy-start | bytes 49156
  7.5 33.4 %collective-permute-start.3 = (f32[6,64,256]{2,1,0:T(8,128)S(1)}, f32[6,64,256]{2,1,0:T(8,128)S(1)}, u32[]{:S(2)}, u32[]{:S(2)}) collective-permute-start(f32[6,64,256]{2,1,0:T(8,128)S(1)} %up.1), channel_id=1, source_target_pairs={{0,1},{1,0},{2,3},{3,2},{4,5},{5,4},{6,7},{7,6},{8,9},{9,8},{10,11... | collective-permute-start | bytes 1179656 | tf_op jit(solution)/shard_map/ppermute | solution.py:415
  10.9 13.2 %collective-permute-start.1 = (s32[8,4]{1,0:T(8,128)S(1)}, s32[8,4]{1,0:T(8,128)S(1)}, u32[]{:S(2)}, u32[]{:S(2)}) collective-permute-start(s32[8,4]{1,0:T(8,128)S(1)} %copy.25.pairs), channel_id=1, source_target_pairs={{0,1},{1,2},{2,3},{3,4},{4,5},{5,6},{6,7},{7,8},{8,9},{9,10},{10,1... | collective-permute-start | bytes 392 | tf_op jit(solution)/shard_map/ppermute | solution.py:421
  21.6 37.1 %collective-permute-start = (bf16[128,4096]{1,0:T(8,128)(2,1)S(1)}, bf16[128,4096]{1,0:T(8,128)(2,1)S(1)}, u32[]{:S(2)}, u32[]{:S(2)}) collective-permute-start(bf16[128,4096]{1,0:T(8,128)(2,1)S(1)} %get-tuple-element.11.stack.other), channel_id=1, source_target_pairs={{1,0},{2,1},{3,2},{4,3},{5,4},{6,5},{7,6},{8,7},{9,8},{10,9},{11,1... | collective-permute-start | bytes 3145736 | tf_op jit(solution)/shard_map/ppermute | solution.py:421
  40.9 8.1 %collective-permute-start.4 = (f32[5,64,256]{2,1,0:T(8,128)S(1)}, f32[5,64,256]{2,1,0:T(8,128)S(1)}, u32[]{:S(2)}, u32[]{:S(2)}) collective-permute-start(f32[5,64,256]{2,1,0:T(8,128)S(1)} %slice.41), channel_id=1, source_target_pairs={{0,2},{1,3},{2,0},{3,1},{4,6},{5,7},{6,4},{7,5},{8,10},{9,11},{10,... | collective-permute-start | bytes 983048 | tf_op jit(solution)/shard_map/ppermute | solution.py:415
  49.1 9.5 %collective-permute-start.5 = (f32[4,64,256]{2,1,0:T(8,128)S(1)}, f32[4,64,256]{2,1,0:T(8,128)S(1)}, u32[]{:S(2)}, u32[]{:S(2)}) collective-permute-start(f32[4,64,256]{2,1,0:T(8,128)S(1)} %slice.43), channel_id=1, source_target_pairs={{0,4},{1,5},{2,6},{3,7},{4,0},{5,1},{6,2},{7,3},{8,12},{9,13},{10,... | collective-permute-start | bytes 786440 | tf_op jit(solution)/shard_map/ppermute | solution.py:415
  58.6 5.7 %collective-permute-start.6 = (f32[3,64,256]{2,1,0:T(8,128)S(1)}, f32[3,64,256]{2,1,0:T(8,128)S(1)}, u32[]{:S(2)}, u32[]{:S(2)}) collective-permute-start(f32[3,64,256]{2,1,0:T(8,128)S(1)} %slice.45), channel_id=1, source_target_pairs={{0,8},{1,9},{2,10},{3,11},{4,12},{5,13},{6,14},{7,15},{8,0},{9,1},... | collective-permute-start | bytes 589832 | tf_op jit(solution)/shard_map/ppermute | solution.py:415
  64.4 9.3 %collective-permute-start.7 = (f32[2,64,256]{2,1,0:T(8,128)S(1)}, f32[2,64,256]{2,1,0:T(8,128)S(1)}, u32[]{:S(2)}, u32[]{:S(2)}) collective-permute-start(f32[2,64,256]{2,1,0:T(8,128)S(1)} %slice.47), channel_id=1, source_target_pairs={{0,16},{1,17},{2,18},{3,19},{4,20},{5,21},{6,22},{7,23},{8,24},{9,... | collective-permute-start | bytes 393224 | tf_op jit(solution)/shard_map/ppermute | solution.py:415
  73.8 7.2 %collective-permute-start.8 = (f32[1,64,256]{2,1,0:T(8,128)S(1)}, f32[1,64,256]{2,1,0:T(8,128)S(1)}, u32[]{:S(2)}, u32[]{:S(2)}) collective-permute-start(f32[1,64,256]{2,1,0:T(8,128)S(1)} %slice.49), channel_id=1, source_target_pairs={{0,32},{1,33},{2,34},{3,35},{4,36},{5,37},{6,38},{7,39},{8,40},{9,... | collective-permute-start | bytes 196616 | tf_op jit(solution)/shard_map/ppermute | solution.py:415
  81.0 18.2 %copy-start.6 = (f32[6,256,256]{2,1,0:T(8,128)S(1)}, f32[6,256,256]{2,1,0:T(8,128)}, u32[]{:S(2)}) copy-start(f32[6,256,256]{2,1,0:T(8,128)} %couplings.1) | copy-start | bytes 4718596
  81.0 18.2 %copy-start.8 = (f32[5,256,256]{2,1,0:T(8,128)S(1)}, f32[5,256,256]{2,1,0:T(8,128)}, u32[]{:S(2)}) copy-start(f32[5,256,256]{2,1,0:T(8,128)} %transfers.3) | copy-start | bytes 3932164
  81.0 12.9 %collective-permute-start.9 = (f32[1,64,256]{2,1,0:T(8,128)S(1)}, f32[1,64,256]{2,1,0:T(8,128)S(1)}, u32[]{:S(2)}, u32[]{:S(2)}) collective-permute-start(f32[1,64,256]{2,1,0:T(8,128)S(1)} %get-tuple-element.17), channel_id=1, source_target_pairs={{0,64},{1,65},{2,66},{3,67},{4,68},{5,69},{6,70},{7,71},{8,72},{9,... | collective-permute-start | bytes 196616 | tf_op jit(solution)/shard_map/ppermute | solution.py:415
  86.0 17.3 %collective-permute-start.2 = (bf16[8,64,512]{2,1,0:T(8,128)(2,1)S(1)}, bf16[8,64,512]{2,1,0:T(8,128)(2,1)S(1)}, u32[]{:S(2)}, u32[]{:S(2)}) collective-permute-start(bf16[8,64,512]{2,1,0:T(8,128)(2,1)S(1)} %get-tuple-element.14), channel_id=1, source_target_pairs={{0,1},{1,2},{2,3},{3,4},{4,5},{5,6},{6,7},{7,8},{8,9},{9,10},{10,1... | collective-permute-start | bytes 1572872 | tf_op jit(solution)/shard_map/ppermute | solution.py:421
  94.0 5.2 %collective-permute-start.10 = (f32[1,64,256]{2,1,0:T(8,128)S(1)}, f32[1,64,256]{2,1,0:T(8,128)S(1)}, u32[]{:S(2)}, u32[]{:S(2)}) collective-permute-start(f32[1,64,256]{2,1,0:T(8,128)S(1)} %add.30), channel_id=1, source_target_pairs={{0,128},{1,129},{2,130},{3,131},{4,132},{5,133},{6,134},{7,135},{8... | collective-permute-start | bytes 196616 | tf_op jit(solution)/shard_map/ppermute | solution.py:415
  99.2 4.1 %copy-start.2 = (f32[64,4096]{1,0:T(8,128)S(1)}, f32[64,4096]{1,0:T(8,128)}, u32[]{:S(2)}) copy-start(f32[64,4096]{1,0:T(8,128)} %residual.3) | copy-start | bytes 3145732
  99.2 4.1 %copy-start.5 = (bf16[256,4096]{1,0:T(8,128)(2,1)S(1)}, bf16[256,4096]{1,0:T(8,128)(2,1)}, u32[]{:S(2)}) copy-start(bf16[256,4096]{1,0:T(8,128)(2,1)} %basis.3) | copy-start | bytes 6291460
  103.3 27.3 %copy-start.3 = (f32[64,4096]{1,0:T(8,128)S(1)}, f32[64,4096]{1,0:T(8,128)}, u32[]{:S(2)}) copy-start(f32[64,4096]{1,0:T(8,128)} %solution.1) | copy-start | bytes 3145732
